TPU v7x, 256 devices: a whole 4x4x8 slice. The times are simulated.
256 devices in a mesh: dp: 32 (over x, z_hi, y), col: 8 (over z_lo, core).
Axes of the slice: x: 4, y: 4, z: 8 (z_hi: 2, z_lo: 4; z = z_hi * 4 + z_lo), core: 2. Of those that a mesh axis runs over, the one named last changes fastest.
Arguments:
- embeddings: bfloat16 [16384, 4096], P('dp'), may hold values from -16 to 16
- rotation: bfloat16 [4096, 4096], P(None, 'col'), may hold values from -0.09375 to 0.09375
- codes: int32 [16384, 512], P('dp', 'col'), may hold values from 0 to 255
- codebooks: bfloat16 [512, 256, 8], P('col'), may hold values from -16 to 16
Outputs:
- new_rotation: float32 [4096, 4096], P('dp', 'col')
All inputs are finite; a program needn't handle non-finite values.
Results may differ from a plain program's by a relative error of at most 0.015.
Values may be sent and summed in bfloat16 or wider, within the bound.
A program may use at most 64 MiB of HBM per device.

v0:
```python
import math
import jax
import jax.numpy as jnp
from jax import lax
from jax.sharding import PartitionSpec as P

STEPS = 2


def rebuild_rows(codes, codebooks):
    tok_rows, sub_count = codes.shape
    centroids = codebooks.shape[1]
    sub_width = codebooks.shape[2]
    group_size = min(16, sub_count)
    centroid_ids = jnp.arange(centroids, dtype=jnp.int32)
    diag_eye = jnp.eye(group_size, dtype=jnp.bfloat16)
    pieces = []
    for first_sub in range(0, sub_count, group_size):
        sub_ids = codes[:, first_sub : first_sub + group_size]
        onehot = (sub_ids[:, :, None] == centroid_ids[None, None, :]).astype(jnp.bfloat16)
        onehot = onehot.reshape(tok_rows, group_size * centroids)
        block_table = (
            codebooks[first_sub : first_sub + group_size][:, :, None, :]
            * diag_eye[:, None, :, None]
        )
        block_table = block_table.reshape(group_size * centroids, group_size * sub_width)
        pieces.append(
            jnp.dot(onehot, block_table, preferred_element_type=jnp.float32).astype(jnp.bfloat16)
        )
    return jnp.concatenate(pieces, axis=1)


def contract_rows(left_rows, right_rows):
    return lax.dot_general(
        left_rows, right_rows, (((0,), (0,)), ((), ())), preferred_element_type=jnp.float32
    )


def shards(embeddings, rotation, codes, codebooks):
    tok_rows, model_width = embeddings.shape
    rows_total = tok_rows * lax.axis_size("dp")
    block_rows = model_width // lax.axis_size("dp")
    rotated = jnp.dot(embeddings, rotation, preferred_element_type=jnp.float32)
    rebuilt = rebuild_rows(codes, codebooks)
    rebuilt_wide = rebuilt.astype(jnp.float32)
    residue = rotated - rebuilt_wide
    partial_value = jnp.sum(residue * residue, axis=1)
    row_error = lax.psum(partial_value, "col")
    weights = 1.0 / (1.0 + row_error / (2.0 * model_width))
    weighted = (weights[:, None] * rebuilt_wide).astype(jnp.bfloat16)
    cross_block = lax.psum_scatter(
        contract_rows(embeddings, weighted), "dp", scatter_dimension=0, tiled=True
    )
    start_row = lax.axis_index("dp") * block_rows
    prior_block = lax.dynamic_slice_in_dim(rotation, start_row, block_rows, 0).astype(jnp.float32)
    cross_block = cross_block + 0.2 * rows_total * prior_block
    frob_total = lax.psum(jnp.sum(cross_block * cross_block), ("dp", "col"))
    norm_scale = 1.4 * jnp.sqrt(frob_total / model_width)
    iterate = cross_block / norm_scale
    for step_index in range(STEPS):
        half_iter = iterate.astype(jnp.bfloat16)
        row_panel = lax.all_gather(half_iter, "col", axis=1, tiled=True)
        gram_block = lax.psum_scatter(
            contract_rows(row_panel, half_iter).astype(jnp.bfloat16),
            "dp",
            scatter_dimension=0,
            tiled=True,
        )
        product = jnp.dot(
            row_panel,
            lax.all_gather(gram_block, "dp", axis=0, tiled=True),
            preferred_element_type=jnp.float32,
        )
        iterate = 1.5 * iterate - 0.5 * product
    return math.sqrt(model_width) * iterate


def solution(mesh):
    placed = (P("dp", None), P(None, "col"), P("dp", "col"), P("col", None, None))
    return jax.shard_map(
        shards, mesh=mesh, in_specs=placed, out_specs=P("dp", "col"), check_vma=False
    )
```

profile of v0, /device:TPU:32, one launch (start us, length us, event | category | flops | bytes accessed | tf_op | source)
XLA Modules:
  0.0 1196.8 jit_solution(9498834475879376770)
XLA Ops:
  6.5 1.0 fusion.12
  7.6 0.4 multiply_bitcast_fusion.3
  8.0 1.4 copy.37
  9.4 0.1 copy.21
  9.6 3.0 iota_compare_fusion.1
  12.6 2.9 copy.36
  15.5 1.5 copy.35
  17.0 0.1 copy.19
  17.1 3.0 iota_compare_fusion.2
  20.1 2.9 copy.34
  23.0 1.5 copy.33
  24.5 0.1 copy.17
  24.6 3.0 iota_compare_fusion.3
  27.6 3.0 copy.32
  30.6 1.4 copy.39
  32.0 0.1 copy.23
  32.1 3.2 iota_compare_fusion
  35.3 1.6 copy.38
  36.9 2.9 convolution_convert_fusion.3
  39.9 1.5 convolution_convert_fusion.4
  41.4 0.0 copy-done.5
  41.4 0.3 copy-done.8
  41.7 1.5 convolution_convert_fusion.5
  43.3 1.5 convolution_convert_fusion.2
  44.8 0.6 copy-done.1
  45.4 1.3 copy-done.11
  46.7 2.4 fusion.1
  49.1 13.7 %psum.14 = f32[512]{0:T(512)S(1)} all-reduce(f32[512]{0:T(512)S(1)} %fusion.1), channel_id=1, replica_groups=mesh['dp'=32,'col'=8] {'col'}, use_global_device_ids=true, to_apply=%region_1.0 | all-reduce | flops 512 | bytes 4096 | tf_op jit(solution)/shard_map/psum | solution.py:48
  62.8 7.8 convolution_bitcast_fusion
  70.7 0.9 constant_dynamic-slice_fusion
  71.6 0.1 copy.31
  71.7 268.2 %reduce-scatter.4.cloned.1.call-done = f32[128,512]{0,1:T(8,128)} async-done(((f32[4096,512]{0,1:T(8,128)}), f32[128,512]{0,1:T(8,128)}) %reduce-scatter.4.cloned.1.call-update) | async-done | bytes 262160 | tf_op jit(solution)/shard_map/reduce_scatter | solution.py:51
  339.9 1.6 multiply_reduce_fusion
  341.5 73.1 %psum.15 = f32[]{:T(128)} all-reduce(f32[]{:T(128)} %multiply_reduce_fusion), channel_id=1, replica_groups=mesh['dp'=32,'col'=8] {'dp','col'}, use_global_device_ids=true, to_apply=%region_4.0 | all-reduce | flops 1 | bytes 8 | tf_op jit(solution)/shard_map/psum | solution.py:57
  415.3 1.7 fusion.9
  417.0 0.3 reduce-scatter.6.cloned.1.call-start
  417.2 30.9 %all-gather.5.cloned.1.call-done = bf16[128,4096]{0,1:T(8,128)(2,1)} async-done(((bf16[128,512]{0,1:T(8,128)(2,1)}), bf16[128,4096]{0,1:T(8,128)(2,1)}) %all-gather.5.cloned.1.call-update) | async-done | bytes 1048592 | tf_op jit(solution)/shard_map/all_gather | solution.py:62
  448.1 4.4 convolution_convert_fusion.1
  452.7 240.5 %reduce-scatter.6.cloned.1.call-done = bf16[128,512]{1,0:T(8,128)(2,1)} async-done(((bf16[4096,512]{1,0:T(8,128)(2,1)}), bf16[128,512]{1,0:T(8,128)(2,1)}) %reduce-scatter.6.cloned.1.call-update) | async-done | bytes 131088 | tf_op jit(solution)/shard_map/reduce_scatter | solution.py:63
  693.2 106.7 %all-gather.7.cloned.1.call-done = bf16[4096,512]{1,0:T(8,128)(2,1)} async-done(((bf16[128,512]{1,0:T(8,128)(2,1)}), bf16[4096,512]{1,0:T(8,128)(2,1)}) %all-gather.7.cloned.1.call-update) | async-done | bytes 4194320 | tf_op jit(solution)/shard_map/all_gather | solution.py:71
  799.9 4.6 fusion.14
  804.5 0.0 reduce-scatter.8.cloned.1.call-start
  804.6 28.6 %all-gather.9.cloned.1.call-done = bf16[128,4096]{0,1:T(8,128)(2,1)} async-done(((bf16[128,512]{0,1:T(8,128)(2,1)}), bf16[128,4096]{0,1:T(8,128)(2,1)}) %all-gather.9.cloned.1.call-update) | async-done | bytes 1048592 | tf_op jit(solution)/shard_map/all_gather | solution.py:62
  833.1 4.4 convolution_convert_fusion
  837.7 239.7 %reduce-scatter.8.cloned.1.call-done = bf16[128,512]{1,0:T(8,128)(2,1)} async-done(((bf16[4096,512]{1,0:T(8,128)(2,1)}), bf16[128,512]{1,0:T(8,128)(2,1)}) %reduce-scatter.8.cloned.1.call-update) | async-done | bytes 131088 | tf_op jit(solution)/shard_map/reduce_scatter | solution.py:63
  1077.4 107.8 %all-gather.11.cloned.1.call-done = bf16[4096,512]{1,0:T(8,128)(2,1)} async-done(((bf16[128,512]{1,0:T(8,128)(2,1)}), bf16[4096,512]{1,0:T(8,128)(2,1)}) %all-gather.11.cloned.1.call-update) | async-done | bytes 4194320 | tf_op jit(solution)/shard_map/all_gather | solution.py:71
  1185.2 3.9 fusion.3
  1189.1 0.8 copy.28
  (39 shorter events, 0.4 us)
Async XLA Ops:
  6.5 2.9 copy-start.10
  6.5 333.3 %reduce-scatter.4.cloned.1.call-start = ((), (), s32[]{:S(2)}) async-start(), calls=%async_computation.3 | async-start | bytes 8650752 | tf_op jit(solution)/shard_map/reduce_scatter | solution.py:51
  30.6 6.3 copy-start.3
  36.9 2.9 copy-start.4
  36.9 2.9 copy-start.7
  39.8 1.6 copy-start.5
  39.8 1.8 copy-start.8
  41.7 1.5 copy-start.9
  43.2 2.2 copy-start.1
  43.2 3.5 copy-start.11
  70.6 377.5 %all-gather.5.cloned.1.call-start = ((), (), s32[]{:S(2)}) async-start(), calls=%async_computation.4 | async-start | bytes 1179648 | tf_op jit(solution)/shard_map/all_gather | solution.py:62
  417.0 276.2 %reduce-scatter.6.cloned.1.call-start = ((), (), s32[]{:S(2)}) async-start(), calls=%async_computation.5 | async-start | bytes 4325376 | tf_op jit(solution)/shard_map/reduce_scatter | solution.py:63
  452.6 347.3 %copy-start.2 = (bf16[128,4096]{0,1:T(8,128)(2,1)S(1)}, bf16[128,4096]{0,1:T(8,128)(2,1)}, u32[]{:S(2)}) copy-start(bf16[128,4096]{0,1:T(8,128)(2,1)} %all-gather.5.cloned.1.call-done) | copy-start | bytes 3145732
  452.6 347.3 %copy-start.6 = (f32[128,512]{0,1:T(8,128)S(1)}, f32[128,512]{0,1:T(8,128)}, u32[]{:S(2)}) copy-start(f32[128,512]{0,1:T(8,128)} %reduce-scatter.4.cloned.1.call-done) | copy-start | bytes 786436
  452.6 347.3 %all-gather.7.cloned.1.call-start = ((), (), s32[]{:S(2)}) async-start(), calls=%async_computation.6 | async-start | bytes 4325376 | tf_op jit(solution)/shard_map/all_gather | solution.py:71
  693.2 140.0 %all-gather.9.cloned.1.call-start = ((), (), s32[]{:S(2)}) async-start(), calls=%async_computation.7 | async-start | bytes 1179648 | tf_op jit(solution)/shard_map/all_gather | solution.py:62
  804.5 272.8 %reduce-scatter.8.cloned.1.call-start = ((), (), s32[]{:S(2)}) async-start(), calls=%async_computation.8 | async-start | bytes 4325376 | tf_op jit(solution)/shard_map/reduce_scatter | solution.py:63
  837.6 347.6 %copy-start = (bf16[128,4096]{0,1:T(8,128)(2,1)S(1)}, bf16[128,4096]{0,1:T(8,128)(2,1)}, u32[]{:S(2)}) copy-start(bf16[128,4096]{0,1:T(8,128)(2,1)} %all-gather.9.cloned.1.call-done) | copy-start | bytes 3145732
  837.6 347.5 %all-gather.11.cloned.1.call-start = ((), (), s32[]{:S(2)}) async-start(), calls=%async_computation.9 | async-start | bytes 4325376 | tf_op jit(solution)/shard_map/all_gather | solution.py:71
Sparse Core Ops, SparseCore 0:
  70.7 269.1 reduce-scatter.3
  417.1 31.0 all-gather.4
  452.7 240.3 reduce-scatter.5
  696.5 103.3 all-gather.6
  804.6 28.4 all-gather.8
  837.7 239.5 reduce-scatter.7
  1080.9 104.2 all-gather.10
where the time goes:
time: 1200 us
  waiting for transfers between devices  1020 us (85%)
  blocking collectives  86.8 us (7%)
  matrix products  35 us (3%)
  local copies, waits for them, and re-layouts  21.9 us (2%)
  other arithmetic  15.8 us (1%)
  between operations  14.4 us (1%)
    reduce_scatter x2, waiting for transfers between devices, shards(): lax.psum_scatter(contract_rows(row_panel, half_iter).astype(jnp.bfloat16)...  480 us
    reduce_scatter x1, waiting for transfers between devices, shards(): lax.psum_scatter(contract_rows(embeddings, weighted), 'dp', scatter_dimen...  268 us
    all_gather x2, waiting for transfers between devices, shards(): lax.all_gather(gram_block, 'dp', axis=0, tiled=True)  214 us
    psum x1, blocking collectives, shards(): frob_total = lax.psum(jnp.sum(cross_block * cross_block), ('dp', 'col'))  73.1 us
    all_gather x2, waiting for transfers between devices, shards(): row_panel = lax.all_gather(half_iter, 'col', axis=1, tiled=True)  59.5 us
  transfers between devices with their start and end apart: 7, of which 7 were waited for; matrix products, arithmetic and copies ran while one was open for 0% of the time, Pallas kernels for 0%

commit v1 on v0

--- a/solution.py
+++ b/solution.py
@@ -5,6 +5,13 @@
 from jax.sharding import PartitionSpec as P
 
 STEPS = 2
+
+
+def all_by_exchange(shard, axis, dim):
+    size = lax.axis_size(axis)
+    parts = jnp.stack([shard for _ in range(size)])
+    parts = lax.all_to_all(parts, axis, split_axis=0, concat_axis=0)
+    return jnp.concatenate(parts, axis=dim)
 
 
 def rebuild_rows(codes, codebooks):
@@ -67,9 +74,7 @@
             tiled=True,
         )
         product = jnp.dot(
-            row_panel,
-            lax.all_gather(gram_block, "dp", axis=0, tiled=True),
-            preferred_element_type=jnp.float32,
+            row_panel, all_by_exchange(gram_block, "dp", 0), preferred_element_type=jnp.float32
         )
         iterate = 1.5 * iterate - 0.5 * product
     return math.sqrt(model_width) * iterate

time: 1200 us -> 1140 us (0.950); the launches traced: 1200 us -> 1120 us
  waiting for transfers between devices: 1020 us -> 814 us
  blocking collectives: 86.8 us -> 223 us
    all_gather x2 -> x0, waiting for transfers between devices: 214 us -> none  [shards(): lax.all_gather(gram_block, 'dp', axis=0, tiled=True)]
    all_to_all x0 -> x2, blocking collectives: none -> 131 us  [all_by_exchange(): parts = lax.all_to_all(parts, axis, split_axis=0, concat_axis=0)]
  transfers between devices with their start and end apart: 7 -> 5, of which waited for: 7 -> 5; matrix products, arithmetic and copies ran while one was open for 0% -> 0% of each run, Pallas kernels for 0% -> 0%
where the time goes in v1:
time: 1140 us; the launch traced here: 1120 us
  waiting for transfers between devices  814 us (71%)
  blocking collectives  223 us (20%)
  matrix products  30.7 us (3%)
  local copies, waits for them, and re-layouts  24.5 us (2%)
  other arithmetic  15.8 us (1%)
  between operations  14.1 us (1%)
    reduce_scatter x2, waiting for transfers between devices, shards(): lax.psum_scatter(contract_rows(row_panel, half_iter).astype(jnp.bfloat16)...  490 us
    reduce_scatter x1, waiting for transfers between devices, shards(): lax.psum_scatter(contract_rows(embeddings, weighted), 'dp', scatter_dimen...  261 us
    all_to_all x2, blocking collectives, all_by_exchange(): parts = lax.all_to_all(parts, axis, split_axis=0, concat_axis=0)  131 us
    psum x1, blocking collectives, shards(): frob_total = lax.psum(jnp.sum(cross_block * cross_block), ('dp', 'col'))  77.5 us
    all_gather x2, waiting for transfers between devices, shards(): row_panel = lax.all_gather(half_iter, 'col', axis=1, tiled=True)  63.5 us
  transfers between devices with their start and end apart: 5, of which 5 were waited for; matrix products, arithmetic and copies ran while one was open for 0% of the time, Pallas kernels for 0%

profile of v1, /device:TPU:32, one launch (start us, length us, event | category | flops | bytes accessed | tf_op | source)
XLA Modules:
  0.0 1122.4 jit_solution(6493240587937093548)
XLA Ops:
  6.5 1.0 fusion.12
  7.6 0.4 multiply_bitcast_fusion.3
  8.0 1.4 copy.37
  9.4 0.1 copy.21
  9.6 3.0 iota_compare_fusion.1
  12.6 2.9 copy.36
  15.5 1.4 copy.35
  16.9 0.1 copy.19
  17.1 3.0 iota_compare_fusion.2
  20.1 2.9 copy.34
  23.0 1.5 copy.33
  24.5 0.1 copy.17
  24.6 3.0 iota_compare_fusion.3
  27.6 2.9 copy.32
  30.5 1.4 copy.39
  31.9 0.1 copy.23
  32.0 3.2 iota_compare_fusion
  35.2 1.6 copy.38
  36.9 2.9 convolution_convert_fusion.3
  39.8 1.5 convolution_convert_fusion.4
  41.4 0.3 copy-done.8
  41.6 1.5 convolution_convert_fusion.5
  43.2 1.5 convolution_convert_fusion.2
  44.7 0.6 copy-done.1
  45.4 1.3 copy-done.11
  46.6 2.4 fusion.1
  49.0 13.7 %psum.14 = f32[512]{0:T(512)S(1)} all-reduce(f32[512]{0:T(512)S(1)} %fusion.1), channel_id=1, replica_groups=mesh['dp'=32,'col'=8] {'col'}, use_global_device_ids=true, to_apply=%region_1.0 | all-reduce | flops 512 | bytes 4096 | tf_op jit(solution)/shard_map/psum | solution.py:55
  62.7 7.8 convolution_bitcast_fusion
  70.6 0.9 constant_dynamic-slice_fusion
  71.5 0.1 copy.31
  71.6 260.9 %reduce-scatter.4.cloned.1.call-done = f32[128,512]{0,1:T(8,128)} async-done(((f32[4096,512]{0,1:T(8,128)}), f32[128,512]{0,1:T(8,128)}) %reduce-scatter.4.cloned.1.call-update) | async-done | bytes 262160 | tf_op jit(solution)/shard_map/reduce_scatter | solution.py:58
  332.5 1.6 multiply_reduce_fusion
  334.2 77.5 %psum.15 = f32[]{:T(128)} all-reduce(f32[]{:T(128)} %multiply_reduce_fusion), channel_id=1, replica_groups=mesh['dp'=32,'col'=8] {'dp','col'}, use_global_device_ids=true, to_apply=%region_4.0 | all-reduce | flops 1 | bytes 8 | tf_op jit(solution)/shard_map/psum | solution.py:64
  412.4 1.7 fusion.9
  414.1 0.3 reduce-scatter.6.cloned.1.call-start
  414.3 31.8 %all-gather.3.cloned.1.call-done = bf16[128,4096]{0,1:T(8,128)(2,1)} async-done(((bf16[128,512]{0,1:T(8,128)(2,1)}), bf16[128,4096]{0,1:T(8,128)(2,1)}) %all-gather.3.cloned.1.call-update) | async-done | bytes 1048592 | tf_op jit(solution)/shard_map/all_gather | solution.py:69
  446.2 4.4 convolution_convert_fusion.1
  450.7 245.5 %reduce-scatter.6.cloned.1.call-done = bf16[128,512]{1,0:T(8,128)(2,1)} async-done(((bf16[4096,512]{1,0:T(8,128)(2,1)}), bf16[128,512]{1,0:T(8,128)(2,1)}) %reduce-scatter.6.cloned.1.call-update) | async-done | bytes 131088 | tf_op jit(solution)/shard_map/reduce_scatter | solution.py:70
  696.2 1.4 stack.4
  697.6 74.6 %all_to_all.10 = bf16[32,128,512]{2,1,0:T(8,128)(2,1)S(1)} all-to-all(bf16[32,128,512]{2,1,0:T(8,128)(2,1)S(1)} %stack.4), channel_id=1, replica_groups=mesh['dp'=32,'col'=8] {'dp'}, dimensions={0} | all-to-all | bytes 8388608 | tf_op jit(solution)/shard_map/all_to_all | solution.py:13
  772.2 2.4 fusion.14
  774.7 31.7 %all-gather.5.cloned.1.call-done = bf16[128,4096]{0,1:T(8,128)(2,1)} async-done(((bf16[128,512]{0,1:T(8,128)(2,1)}), bf16[128,4096]{0,1:T(8,128)(2,1)}) %all-gather.5.cloned.1.call-update) | async-done | bytes 1048592 | tf_op jit(solution)/shard_map/all_gather | solution.py:69
  806.4 4.4 convolution_convert_fusion
  810.8 244.3 %reduce-scatter.8.cloned.1.call-done = bf16[128,512]{1,0:T(8,128)(2,1)} async-done(((bf16[4096,512]{1,0:T(8,128)(2,1)}), bf16[128,512]{1,0:T(8,128)(2,1)}) %reduce-scatter.8.cloned.1.call-update) | async-done | bytes 131088 | tf_op jit(solution)/shard_map/reduce_scatter | solution.py:70
  1055.1 1.4 stack.5
  1056.5 56.7 %all_to_all.11 = bf16[32,128,512]{2,1,0:T(8,128)(2,1)S(1)} all-to-all(bf16[32,128,512]{2,1,0:T(8,128)(2,1)S(1)} %stack.5), channel_id=1, replica_groups=mesh['dp'=32,'col'=8] {'dp'}, dimensions={0} | all-to-all | bytes 8388608 | tf_op jit(solution)/shard_map/all_to_all | solution.py:13
  1113.2 1.8 fusion.3
  1115.0 0.8 copy.28
  (37 shorter events, 0.4 us)
Async XLA Ops:
  6.5 2.9 copy-start.10
  6.5 326.0 %reduce-scatter.4.cloned.1.call-start = ((), (), s32[]{:S(2)}) async-start(), calls=%async_computation.5 | async-start | bytes 8650752 | tf_op jit(solution)/shard_map/reduce_scatter | solution.py:58
  30.5 6.3 copy-start.3
  36.8 2.9 copy-start.4
  36.8 2.9 copy-start.7
  39.8 1.6 copy-start.5
  39.8 1.8 copy-start.8
  41.6 1.5 copy-start.9
  43.2 2.2 copy-start.1
  43.2 3.5 copy-start.11
  70.5 375.6 %all-gather.3.cloned.1.call-start = ((), (), s32[]{:S(2)}) async-start(), calls=%async_computation.6 | async-start | bytes 1179648 | tf_op jit(solution)/shard_map/all_gather | solution.py:69
  414.1 282.1 %reduce-scatter.6.cloned.1.call-start = ((), (), s32[]{:S(2)}) async-start(), calls=%async_computation.7 | async-start | bytes 4325376 | tf_op jit(solution)/shard_map/reduce_scatter | solution.py:70
  450.6 355.8 %all-gather.5.cloned.1.call-start = ((), (), s32[]{:S(2)}) async-start(), calls=%async_computation.8 | async-start | bytes 1179648 | tf_op jit(solution)/shard_map/all_gather | solution.py:69
  697.6 74.6 %copy-start.2 = (bf16[128,4096]{0,1:T(8,128)(2,1)S(1)}, bf16[128,4096]{0,1:T(8,128)(2,1)}, u32[]{:S(2)}) copy-start(bf16[128,4096]{0,1:T(8,128)(2,1)} %all-gather.3.cloned.1.call-done) | copy-start | bytes 3145732
  697.6 74.6 %copy-start.6 = (f32[128,512]{0,1:T(8,128)S(1)}, f32[128,512]{0,1:T(8,128)}, u32[]{:S(2)}) copy-start(f32[128,512]{0,1:T(8,128)} %reduce-scatter.4.cloned.1.call-done) | copy-start | bytes 786436
  774.6 280.5 %reduce-scatter.8.cloned.1.call-start = ((), (), s32[]{:S(2)}) async-start(), calls=%async_computation.9 | async-start | bytes 4325376 | tf_op jit(solution)/shard_map/reduce_scatter | solution.py:70
  1056.5 56.7 %copy-start = (bf16[128,4096]{0,1:T(8,128)(2,1)S(1)}, bf16[128,4096]{0,1:T(8,128)(2,1)}, u32[]{:S(2)}) copy-start(bf16[128,4096]{0,1:T(8,128)(2,1)} %all-gather.5.cloned.1.call-done) | copy-start | bytes 3145732
Sparse Core Ops, SparseCore 0:
  70.6 261.8 reduce-scatter.3
  414.2 31.9 all-gather.2
  450.7 245.4 reduce-scatter.5
  774.7 31.5 all-gather.4
  811.0 244.1 reduce-scatter.7
